TPU v7x, 256 devices: a whole 4x4x8 slice. The times are simulated.
256 devices in a mesh: seq: 32 (over y, x, core), tp: 8 (over z).
Axes of the slice: x: 4, y: 4, z: 8, core: 2. Of those that a mesh axis runs over, the one named last changes fastest.
Arguments:
- queries: bfloat16 [32, 64, 4096], P('seq', None, 'tp'), may hold values from -8 to 8
- draft_kv: bfloat16 [32, 64, 8, 128], P('seq', None, 'tp'), may hold values from -12.5 to 12.5
- cache_kv: bfloat16 [8, 16384, 8, 128], P(None, 'seq', 'tp'), may hold values from -10 to 10
- cache_len: int32 [8], replicated, may hold values from 4096 to 16384
- group_of: int32 [32], replicated, may hold values from 0 to 7, as said below
- parents: int32 [32, 64], P('seq'), may hold values from 0 to 62, as said below
- sink_logit: float32 [64], P('tp'), may hold values from 4 to 20
- w_out: bfloat16 [4096, 2880], P('tp'), may hold values from -0.09375 to 0.09375
- hidden_in: bfloat16 [2048, 2880], P('seq', 'tp'), may hold values from -3 to 3
- norm_gain: float32 [2880], replicated, may hold values from 0.5 to 1.5
- routes: int32 [2048, 4], P('seq'), may hold values from 0 to 31, all different within a row; in each aligned block of 64 rows (0 to 63, 64 to 127, ...) at most 16 rows name the same one
- route_weight: float32 [2048, 4], P('seq'), may hold values from 0.1 to 1
- w_gate_up: bfloat16 [32, 2, 2880, 2880], P('seq', None, None, 'tp'), may hold values from -0.109375 to 0.109375
- w_down: bfloat16 [32, 2880, 2880], P('seq', 'tp'), may hold values from -0.109375 to 0.109375
- accepted_idx: int32 [32, 16], P('seq'), may hold values from 0 to 45, as said below
- accepted_len: int32 [32], P('seq'), may hold values from 1 to 16, as said below
- tail_slot: int32 [32], replicated, may hold values from 0 to 31, each once
Outputs:
- out_hidden: bfloat16 [2048, 2880], P('seq', 'tp')
- new_tail: bfloat16 [32, 16, 8, 128], P('seq', None, 'tp')
Inputs may be any that keep to these rules, and one draw needn't show every extreme that they name: `parents`: node 0 of every tree is its root and its own parent; every other node's parent is one of the three nodes before it. `accepted_idx`: row r lists the first 16 nodes of a path from the root of request r's tree down to one of its last four nodes, root first. `accepted_len`: each request accepts one or more nodes. `group_of`: every prompt group has exactly 4 requests. `routes`: the 4 experts of a token differ; at most 16 of one device's rows (one aligned block of 64 tokens) name one expert.
All inputs are finite; a program needn't handle non-finite values.
Results may differ from a plain program's by a relative error of at most 0.025.
Values may be sent and summed in bfloat16 or wider, within the bound.
A program may use at most 128 MiB of HBM per device.

v0:
```python
import jax
import jax.numpy as jnp
from jax import lax
from jax.sharding import PartitionSpec as P

HQ = 64
KVH = 8
HD = 64


def ancestry(parents):
    tree_len = parents.shape[1]
    node_ids = jnp.arange(tree_len, dtype=jnp.int32)
    linked = (parents[:, :, None] == node_ids[None, None, :]) | (
        node_ids[:, None] == node_ids[None, :]
    )[None]
    reachable = linked.astype(jnp.float32)
    for repeat in range((tree_len - 1).bit_length()):
        reachable = jnp.minimum(
            jnp.einsum("rij,rjk->rik", reachable, reachable, precision=lax.Precision.HIGHEST), 1.0
        )
    return reachable


def cache_block(block_queries, block_groups, cache_kv, cache_len, positions):
    block_rows, tree_len, head_cols = block_queries.shape
    kv_dev = cache_kv.shape[2]
    grouped = block_queries.reshape(block_rows, tree_len, kv_dev, HQ // KVH, HD)
    picked = jnp.take(cache_kv, block_groups, axis=0)
    cache_keys = picked[..., :HD]
    cache_values = picked[..., HD:]
    scores = (
        jnp.einsum("rtkqd,rckd->rkqtc", grouped, cache_keys, preferred_element_type=jnp.float32)
        * 0.125
    )
    lengths = jnp.take(cache_len, block_groups)
    usable = (positions[None, :] < lengths[:, None])[:, None, None, None, :]
    masked = jnp.where(usable, scores, -1e30)
    shard_max = jnp.max(masked, axis=-1)
    weights = jnp.where(usable, jnp.exp(masked - shard_max[..., None]), 0.0)
    shard_sum = jnp.sum(weights, axis=-1)
    shard_out = jnp.einsum(
        "rkqtc,rckd->rkqtd",
        weights.astype(jnp.bfloat16),
        cache_values,
        preferred_element_type=jnp.float32,
    )
    shard_out = (shard_out / jnp.maximum(shard_sum, 1.0)[..., None]).astype(jnp.bfloat16)
    out_rows = shard_out.transpose(0, 3, 1, 2, 4).reshape(block_rows, tree_len, head_cols)
    max_rows = shard_max.transpose(0, 3, 1, 2).reshape(block_rows, tree_len, -1)
    sum_rows = shard_sum.transpose(0, 3, 1, 2).reshape(block_rows, tree_len, -1)
    return (out_rows, max_rows, sum_rows)


def expert_rows(arrived, w_gate_up, w_down):
    exp_dev = w_gate_up.shape[0]
    sources = arrived.shape[0] // exp_dev
    grouped = arrived.reshape(sources, exp_dev, arrived.shape[1], arrived.shape[2])
    gate_proj = jnp.einsum(
        "sexd,edf->sexf", grouped, w_gate_up[:, 0], preferred_element_type=jnp.float32
    )
    upward = jnp.einsum(
        "sexd,edf->sexf", grouped, w_gate_up[:, 1], preferred_element_type=jnp.float32
    )
    active = (gate_proj * jax.nn.sigmoid(1.702 * gate_proj) * (upward + 1.0)).astype(jnp.bfloat16)
    down_part = jnp.einsum("sexf,efd->sexd", active, w_down, preferred_element_type=jnp.float32)
    return down_part.reshape(arrived.shape[0], arrived.shape[1], -1)


def shards(
    queries,
    draft_kv,
    cache_kv,
    cache_len,
    group_of,
    parents,
    sink_logit,
    w_out,
    hidden_in,
    norm_gain,
    routes,
    route_weight,
    w_gate_up,
    w_down,
    accepted_idx,
    accepted_len,
    tail_slot,
):
    seq_count = lax.axis_size("seq")
    req_dev, tree_len, head_cols = queries.shape
    kv_dev = cache_kv.shape[2]
    per_kv = HQ // KVH
    heads_dev = kv_dev * per_kv
    shard_len = cache_kv.shape[1]
    positions = lax.axis_index("seq") * shard_len + jnp.arange(shard_len, dtype=jnp.int32)
    every_query = lax.all_gather(queries, "seq", axis=0, tiled=True)
    requests_all = every_query.shape[0]
    block_count = requests_all // 8
    stacked = (
        every_query.reshape(block_count, 8, tree_len, head_cols),
        group_of.reshape(block_count, 8),
    )
    shard_out, shard_max, shard_sum = lax.map(
        lambda blocks: cache_block(blocks[0], blocks[1], cache_kv, cache_len, positions), stacked
    )
    shard_out = shard_out.reshape(seq_count, req_dev, tree_len, head_cols)
    shard_max = shard_max.reshape(seq_count, req_dev, tree_len, heads_dev)
    shard_sum = shard_sum.reshape(seq_count, req_dev, tree_len, heads_dev)
    came_out = lax.all_to_all(shard_out, "seq", split_axis=0, concat_axis=0, tiled=True)
    came_max, came_sum = (
        lax.all_to_all(shard_max, "seq", split_axis=0, concat_axis=0, tiled=True),
        lax.all_to_all(shard_sum, "seq", split_axis=0, concat_axis=0, tiled=True),
    )
    reachable = ancestry(parents)
    own_heads = queries.reshape(req_dev, tree_len, kv_dev, per_kv, HD)
    draft_keys = draft_kv[..., :HD]
    draft_values = draft_kv[..., HD:]
    tree_scores = (
        jnp.einsum("rtkqd,rukd->rkqtu", own_heads, draft_keys, preferred_element_type=jnp.float32)
        * 0.125
    )
    allowed = (reachable > 0.5)[:, None, None, :, :]
    tree_masked = jnp.where(allowed, tree_scores, -1e30)
    tree_max = jnp.max(tree_masked, axis=-1)
    tree_weight = jnp.where(allowed, jnp.exp(tree_masked - tree_max[..., None]), 0.0)
    tree_sum = jnp.sum(tree_weight, axis=-1)
    tree_num = jnp.einsum(
        "rkqtu,rukd->rkqtd",
        tree_weight.astype(jnp.bfloat16),
        draft_values,
        preferred_element_type=jnp.float32,
    )
    tree_max = tree_max.transpose(0, 3, 1, 2).reshape(req_dev, tree_len, heads_dev)
    tree_sum = tree_sum.transpose(0, 3, 1, 2).reshape(req_dev, tree_len, heads_dev)
    tree_num = tree_num.transpose(0, 3, 1, 2, 4).reshape(req_dev, tree_len, heads_dev, HD)
    sink_rows = sink_logit[None, None, :]
    ceiling = jnp.maximum(jnp.maximum(jnp.max(came_max, axis=0), tree_max), sink_rows)
    shard_scale = came_sum * jnp.exp(came_max - ceiling[None])
    tree_scale = jnp.exp(tree_max - ceiling)
    denominator = (
        jnp.sum(shard_scale, axis=0) + tree_scale * tree_sum + jnp.exp(sink_rows - ceiling)
    )
    weighted = jnp.sum(
        shard_scale[..., None]
        * came_out.reshape(seq_count, req_dev, tree_len, heads_dev, HD).astype(jnp.float32),
        axis=0,
    )
    numerator = weighted + tree_scale[..., None] * tree_num
    attention = (
        (numerator / denominator[..., None])
        .reshape(req_dev * tree_len, heads_dev * HD)
        .astype(jnp.bfloat16)
    )
    projected = jnp.dot(attention, w_out, preferred_element_type=jnp.float32)
    width_dev = hidden_in.shape[1]
    tp_index = lax.axis_index("tp")
    summed = lax.psum(projected, "tp")
    resid_full = lax.all_gather(hidden_in, "tp", axis=1, tiled=True)
    stream = (resid_full.astype(jnp.float32) + summed).astype(jnp.bfloat16)
    stream_f = stream.astype(jnp.float32)
    inv_scale = lax.rsqrt(jnp.mean(stream_f * stream_f, axis=-1, keepdims=True) + 1e-05)
    normed_full = (stream_f * inv_scale * norm_gain[None, :]).astype(jnp.bfloat16)
    stream_cols = lax.dynamic_slice_in_dim(stream, tp_index * width_dev, width_dev, 1)
    tok_dev = routes.shape[0]
    top_count = routes.shape[1]
    exp_dev = w_gate_up.shape[0]
    experts_all = seq_count * exp_dev
    capacity = 2 * tok_dev * top_count // experts_all
    flat_routes = routes.reshape(-1)
    onehot = (flat_routes[:, None] == jnp.arange(experts_all, dtype=jnp.int32)[None, :]).astype(
        jnp.int32
    )
    position = jnp.sum((jnp.cumsum(onehot, axis=0) - onehot) * onehot, axis=1)
    slot_ids = flat_routes * capacity + position
    buckets = jnp.arange(experts_all * capacity, dtype=jnp.int32)
    placing = jnp.sum(
        (slot_ids.reshape(tok_dev, top_count)[None, :, :] == buckets[:, None, None]).astype(
            jnp.int32
        ),
        axis=2,
    ).astype(jnp.bfloat16)
    dispatched = (
        jnp.dot(placing, normed_full, preferred_element_type=jnp.float32)
        .astype(jnp.bfloat16)
        .reshape(experts_all, capacity, -1)
    )
    down_part = expert_rows(
        lax.all_to_all(dispatched, "seq", split_axis=0, concat_axis=0, tiled=True),
        w_gate_up,
        w_down,
    )
    expert_out = lax.psum_scatter(
        down_part.astype(jnp.bfloat16), "tp", scatter_dimension=2, tiled=True
    )
    returned = lax.all_to_all(expert_out, "seq", split_axis=0, concat_axis=0, tiled=True)
    gathered_rows = jnp.take(
        returned.reshape(experts_all * capacity, -1), slot_ids, axis=0
    ).reshape(tok_dev, top_count, -1)
    mixture = jnp.sum(route_weight[:, :, None] * gathered_rows.astype(jnp.float32), axis=1)
    out_hidden = (stream_cols.astype(jnp.float32) + mixture).astype(jnp.bfloat16)
    blk_len = accepted_idx.shape[1]
    chosen = draft_kv[jnp.arange(req_dev, dtype=jnp.int32)[:, None], accepted_idx]
    kept_rows = jnp.arange(blk_len, dtype=jnp.int32)[None, :] < accepted_len[:, None]
    picked_rows = jnp.where(kept_rows[:, :, None, None], chosen, jnp.zeros_like(chosen))
    everyone = lax.all_gather(picked_rows, "seq", axis=0, tiled=True)
    my_slots = lax.axis_index("seq") * req_dev + jnp.arange(req_dev, dtype=jnp.int32)
    selector = (tail_slot[None, :] == my_slots[:, None]).astype(jnp.bfloat16)
    new_tail = jnp.dot(
        selector, everyone.reshape(everyone.shape[0], -1), preferred_element_type=jnp.float32
    ).astype(jnp.bfloat16)
    new_tail = new_tail.reshape(req_dev, blk_len, kv_dev, -1)
    return (out_hidden, new_tail)


def solution(mesh):
    in_specs = (
        P("seq", None, "tp"),
        P("seq", None, "tp", None),
        P(None, "seq", "tp", None),
        P(),
        P(),
        P("seq", None),
        P("tp"),
        P("tp", None),
        P("seq", "tp"),
        P(),
        P("seq", None),
        P("seq", None),
        P("seq", None, None, "tp"),
        P("seq", "tp", None),
        P("seq", None),
        P("seq"),
        P(),
    )
    out_specs = (P("seq", "tp"), P("seq", None, "tp", None))
    return jax.shard_map(shards, mesh=mesh, in_specs=in_specs, out_specs=out_specs, check_vma=False)
```

profile of v0, /device:TPU:1, one launch (start us, length us, event | category | flops | bytes accessed | tf_op | source)
XLA Modules:
  0.0 533.3 jit_solution(3878875501359007208)
XLA Ops:
  10.3 53.3 %all-gather.3.cloned.1.call-done = bf16[32,64,512]{2,1,0:T(8,128)(2,1)} async-done(((bf16[1,64,512]{2,1,0:T(8,128)(2,1)}), bf16[32,64,512]{2,1,0:T(8,128)(2,1)}) %all-gather.3.cloned.1.call-update) | async-done | bytes 2097168 | tf_op jit(solution)/shard_map/all_gather | solution.py:96
  63.7 97.3 %while.15 = (s32[]{:T(128)}, bf16[4,8,64,512]{3,2,1,0:T(8,128)(2,1)}, f32[4,8,64,8]{2,3,1,0:T(8,128)}, f32[4,8,64,8]{2,3,1,0:T(8,128)}, s32[4,8]{1,0:T(4,128)S(1...) while((s32[]{:T(128)}, ...), condition=%wide.region_3.4_spmd.clone, body=%wide.region_0.3_spmd.clone.sunk | while | flops 565184128 | bytes 43791872 | solution.py:103
  65.0 2.9 gather_fusion.1
  75.3 2.7 bitcast_reduce_fusion.3
  89.4 2.9 gather_fusion.1
  99.6 2.7 bitcast_reduce_fusion.3
  113.7 2.9 gather_fusion.1
  124.0 2.7 bitcast_reduce_fusion.3
  138.0 2.9 gather_fusion.1
  148.3 2.7 bitcast_reduce_fusion.3
  162.7 5.1 all-to-all-start.1
  170.4 4.7 all-to-all-done.1
  175.1 3.9 all-to-all-start
  180.8 5.6 %all-to-all-done = f32[32,1,512]{2,1,0:T(1,128)S(1)} async-done(((f32[32,1,512]{2,1,0:T(1,128)}), f32[32,1,512]{2,1,0:T(1,128)S(1)}, u32[]{:S(2)}, u32[]{:S(2)}) %all-to-all-start) | async-done | bytes 65568 | tf_op jit(solution)/shard_map/all_to_all | solution.py:112
  186.4 4.7 all-to-all-start.2
  193.3 23.3 %all-gather = bf16[8,360,64]{1,2,0:T(8,128)(2,1)S(1)} all-gather(bf16[1,360,64]{1,2,0:T(8,128)(2,1)} %bitcast.318), channel_id=1, replica_groups=mesh['seq'=32,'tp'=8] {'tp'}, dimensions={0}, use_global_device_ids=true | all-gather | bytes 414720 | tf_op jit(solution)/shard_map/all_gather | solution.py:158
  227.4 5.9 %mul.135 = f32[32,64,8,64]{3,2,1,0:T(8,128)} broadcast(f32[32,64,8]{2,1,0:T(8,128)} %copy.92), dimensions={0,1,2} | broadcast | bytes 4259840 | tf_op jit(solution)/shard_map/mul | solution.py:144
  233.4 7.5 %mul.136 = f32[32,1,64,512]{3,2,1,0:T(8,128)} reshape(f32[32,64,8,64]{3,2,1,0:T(8,128)} %mul.135) | data formatting | bytes 8388608 | tf_op jit(solution)/shard_map/mul | solution.py:144
  240.9 3.6 multiply_reduce_fusion
  247.8 72.6 %all-reduce.3.cloned.1.call-done = f32[64,2880]{1,0:T(8,128)} async-done(((f32[64,2880]{1,0:T(8,128)}), f32[64,2880]{1,0:T(8,128)}) %all-reduce.3.cloned.1.call-update) | async-done | bytes 737296 | tf_op jit(solution)/shard_map/psum | solution.py:157
  325.4 4.6 copy.103
  329.9 50.3 %all_to_all.25 = bf16[32,16,2880]{2,1,0:T(8,128)(2,1)S(1)} all-to-all(bf16[32,16,2880]{2,1,0:T(8,128)(2,1)} %bitcast.309), channel_id=1, replica_groups=mesh['seq'=32,'tp'=8] {'seq'}, dimensions={0} | all-to-all | bytes 5898240 | tf_op jit(solution)/shard_map/all_to_all | solution.py:188
  381.9 4.2 fusion.27
  386.1 8.5 %convolution_convert_fusion = bf16[32,16,2880]{2,1,0:T(8,128)(2,1)} fusion(bf16[1,360,2880]{2,1,0:T(8,128)(2,1)} %param.32, bf16[32,16,2880]{2,1,0:T(8,128)(2,1)} %copy-done.2, bf16[1,2,2880,360]{2,3,1,0:T(8,128)(2,1)} %param.31, f32[32,1,16,360]{3,2,0,1:T(8,128)} %fusion.27), kind=kOutput, calls=%fused_computation.40 | convolution fusion | flops 2126315520 | bytes 10989568 | tf_op jit(solution)/shard_map/sexf,efd->sexd/dot_general | solution.py:66
  394.6 21.4 %copy.108 = bf16[32,16,2880]{1,0,2:T(8,128)(2,1)} copy(bf16[32,16,2880]{2,1,0:T(8,128)(2,1)} %convolution_convert_fusion) | data formatting | bytes 5898240
  416.0 39.5 %reshape.749 = bf16[2880,512]{1,0:T(8,128)(2,1)} reshape(bf16[2880,32,16]{2,1,0:T(8,128)(2,1)} %bitcast.306) | data formatting | bytes 5898240
  457.1 22.6 %all_gather.11 = bf16[32,16,1,128]{3,1,2,0:T(8,128)(2,1)S(1)} all-gather(bf16[1,16,1,128]{3,1,2,0:T(8,128)(2,1)S(1)} %bitcast_select_fusion.2), channel_id=1, replica_groups=mesh['seq'=32,'tp'=8] {'seq'}, dimensions={0}, use_global_device_ids=true | all-gather | bytes 135168 | tf_op jit(solution)/shard_map/all_gather | solution.py:205
  479.9 12.3 %reduce-scatter.4.cloned.1.call-done = bf16[360,512]{1,0:T(8,128)(2,1)} async-done(((bf16[2880,512]{1,0:T(8,128)(2,1)}), bf16[360,512]{1,0:T(8,128)(2,1)}) %reduce-scatter.4.cloned.1.call-update) | async-done | bytes 368656
  492.2 4.4 reshape.750
  496.5 5.0 copy.109
  501.6 11.1 %all-to-all-start.4 = ((bf16[32,16,360]{2,1,0:T(8,128)(2,1)}), bf16[32,16,360]{2,1,0:T(8,128)(2,1)S(1)}, u32[]{:S(2)}, u32[]{:S(2)}) async-start(bf16[32,16,360]{2,1,0:T(8,128)(2,1)} %copy.109), calls=%async_computation.4 | async-start | bytes 786432 | tf_op jit(solution)/shard_map/all_to_all | solution.py:195
  514.1 8.7 %all-to-all-done.4 = bf16[32,16,360]{2,1,0:T(8,128)(2,1)S(1)} async-done(((bf16[32,16,360]{2,1,0:T(8,128)(2,1)}), bf16[32,16,360]{2,1,0:T(8,128)(2,1)S(1)}, u32[]{:S(2)}, u32[]{:S(2)}) %all-to-all-start.4) | async-done | bytes 368672 | tf_op jit(solution)/shard_map/all_to_all | solution.py:195
  (194 shorter events, 113.0 us)
Async XLA Ops:
  7.2 237.3 %copy-start = (bf16[512,2880]{0,1:T(8,128)(2,1)S(1)}, bf16[512,2880]{0,1:T(8,128)(2,1)}, u32[]{:S(2)}) copy-start(bf16[512,2880]{0,1:T(8,128)(2,1)} %param.26) | copy-start | bytes 8847364
  7.2 56.5 %all-gather.3.cloned.1.call-start = ((), (), s32[]{:S(2)}) async-start(), calls=%async_computation.6 | async-start | bytes 2162688 | tf_op jit(solution)/shard_map/all_gather | solution.py:96
  63.7 115.5 %copy-start.6 = (bf16[1,64,512]{2,1,0:T(8,128)(2,1)S(1)}, bf16[1,64,512]{2,1,0:T(8,128)(2,1)}, u32[]{:S(2)}) copy-start(bf16[1,64,512]{2,1,0:T(8,128)(2,1)} %param.19) | copy-start | bytes 196612
  63.7 115.6 %copy-start.13 = (s32[64,4]{0,1:T(4,128)S(1)}, s32[64,4]{0,1:T(4,128)}, u32[]{:S(2)}) copy-start(s32[64,4]{0,1:T(4,128)} %param.29) | copy-start | bytes 3076
  78.0 3.0 copy-start.1
  102.3 3.0 copy-start.1
  126.6 3.0 copy-start.1
  150.9 3.0 copy-start.1
  161.0 30.9 %copy-start.7 = (bf16[1,64,1,128]{3,1,2,0:T(8,128)(2,1)S(1)}, bf16[1,64,1,128]{3,1,2,0:T(8,128)(2,1)}, u32[]{:S(2)}) copy-start(bf16[1,64,1,128]{3,1,2,0:T(8,128)(2,1)} %param.20) | copy-start | bytes 49156
  162.7 12.4 %all-to-all-start.1 = ((f32[32,1,512]{2,1,0:T(1,128)}), f32[32,1,512]{2,1,0:T(1,128)S(1)}, u32[]{:S(2)}, u32[]{:S(2)}) async-start(f32[32,1,512]{2,1,0:T(1,128)} %reshape.754), calls=%async_computation.1 | async-start | bytes 131072 | tf_op jit(solution)/shard_map/all_to_all | solution.py:111
  175.1 17.0 %copy-start.9 = (f32[32,1,512]{2,1,0:T(1,128)}, f32[32,1,512]{2,1,0:T(1,128)S(1)}, u32[]{:S(2)}) copy-start(f32[32,1,512]{2,1,0:T(1,128)S(1)} %all-to-all-done.1) | copy-start | bytes 196612
  175.1 11.3 %all-to-all-start = ((f32[32,1,512]{2,1,0:T(1,128)}), f32[32,1,512]{2,1,0:T(1,128)S(1)}, u32[]{:S(2)}, u32[]{:S(2)}) async-start(f32[32,1,512]{2,1,0:T(1,128)} %reshape.752), calls=%async_computation | async-start | bytes 131072 | tf_op jit(solution)/shard_map/all_to_all | solution.py:112
  186.4 4.8 copy-start.11
  186.4 54.4 %all-to-all-start.2 = ((bf16[32,1,64,512]{3,2,1,0:T(8,128)(2,1)}), bf16[32,1,64,512]{3,2,1,0:T(8,128)(2,1)}, u32[]{:S(2)}, u32[]{:S(2)}) async-start(bf16[32,1,64,512]{3,2,1,0:T(8,128)(2,1)} %bitcast.313), calls=%async_computation.2 | async-start | bytes 4194304 | tf_op jit(solution)/shard_map/all_to_all | solution.py:109
  191.2 129.2 %all-reduce.3.cloned.1.call-start = ((), (), s32[]{:S(2)}) async-start(), calls=%async_computation.7 | async-start | bytes 1507328 | tf_op jit(solution)/shard_map/psum | solution.py:157
  192.4 28.8 %copy-start.10 = (f32[32,1,512]{2,1,0:T(1,128)S(1)}, f32[32,1,512]{2,1,0:T(1,128)}, u32[]{:S(2)}) copy-start(f32[32,1,512]{2,1,0:T(1,128)} %copy-done.9) | copy-start | bytes 196612
  193.3 28.8 %copy-start.12 = (f32[32,1,512]{2,1,0:T(1,128)S(1)}, f32[32,1,512]{2,1,0:T(1,128)}, u32[]{:S(2)}) copy-start(f32[32,1,512]{2,1,0:T(1,128)} %copy-done.11) | copy-start | bytes 196612
  240.9 3.6 copy-start.4
  240.9 3.6 copy-start.5
  244.5 2.0 copy-start.16
  244.5 2.8 copy-start.15
  244.5 78.2 %copy-start.14 = (f32[2880]{0:T(1024)S(1)}, f32[2880]{0:T(1024)}, u32[]{:S(2)}) copy-start(f32[2880]{0:T(1024)} %param.28) | copy-start | bytes 34564
  246.4 245.7 %reduce-scatter.4.cloned.1.call-start = ((), (), s32[]{:S(2)}) async-start(), calls=%async_computation.8 | async-start | bytes 3317760
  321.9 0.8 copy-start.3
  380.2 1.6 copy-start.2
  455.4 0.9 copy-start.19
  455.4 1.0 copy-start.8
  455.4 24.3 %copy-start.18 = (s32[32]{0:T(128)S(1)}, s32[32]{0:T(128)}, u32[]{:S(2)}) copy-start(s32[32]{0:T(128)} %param.35) | copy-start | bytes 388
  479.8 33.0 %copy-start.17 = (f32[64,4]{0,1:T(4,128)S(1)}, f32[64,4]{0,1:T(4,128)}, u32[]{:S(2)}) copy-start(f32[64,4]{0,1:T(4,128)} %param.30) | copy-start | bytes 3076
  501.6 21.3 %all-to-all-start.4 = ((bf16[32,16,360]{2,1,0:T(8,128)(2,1)}), bf16[32,16,360]{2,1,0:T(8,128)(2,1)S(1)}, u32[]{:S(2)}, u32[]{:S(2)}) async-start(bf16[32,16,360]{2,1,0:T(8,128)(2,1)} %copy.109), calls=%async_computation.4 | async-start | bytes 786432 | tf_op jit(solution)/shard_map/all_to_all | solution.py:195
Sparse Core Ops, SparseCore 0:
  10.6 53.0 all-gather.2
  246.5 73.8 all-reduce.2
  455.6 36.5 reduce-scatter.3
where the time goes:
time: 536 us; the launch traced here: 533 us
  local copies, waits for them, and re-layouts  164 us (31%)
  waiting for transfers between devices  158 us (29%)
  blocking collectives  96.2 us (18%)
  matrix products  42.4 us (8%)
  other arithmetic  32.4 us (6%)
  starting transfers between devices  25 us (5%)
  between operations  14.9 us (3%)
    unnamed x48, local copies, waits for them, and re-layouts  77 us
    psum x1, waiting for transfers between devices, shards(): summed = lax.psum(projected, 'tp')  72.6 us
    all_gather x1, waiting for transfers between devices, shards(): every_query = lax.all_gather(queries, 'seq', axis=0, tiled=True)  53.3 us
    all_to_all x1, blocking collectives, shards(): lax.all_to_all(dispatched, 'seq', split_axis=0, concat_axis=0, tiled=True)  50.3 us
    all_gather x1, blocking collectives, shards(): resid_full = lax.all_gather(hidden_in, 'tp', axis=1, tiled=True)  23.3 us
    all_gather x1, blocking collectives, shards(): everyone = lax.all_gather(picked_rows, 'seq', axis=0, tiled=True)  22.6 us
    gather x8, local copies, waits for them, and re-layouts, cache_block(): picked = jnp.take(cache_kv, block_groups, axis=0)  20.7 us
    mul x3, local copies, waits for them, and re-layouts, shards(): shard_scale[..., None]  14.9 us
  transfers between devices with their start and end apart: 7, of which 6 were waited for; matrix products, arithmetic and copies ran while one was open for 7% of the time, Pallas kernels for 0%

commit v1 on v0

--- a/solution.py
+++ b/solution.py
@@ -6,6 +6,10 @@
 HQ = 64
 KVH = 8
 HD = 64
+
+
+def detail_loads(load):
+    return jax.lax.all_gather(load, axis_name="tp").sum(axis=0)
 
 
 def ancestry(parents):
@@ -154,7 +158,7 @@
     projected = jnp.dot(attention, w_out, preferred_element_type=jnp.float32)
     width_dev = hidden_in.shape[1]
     tp_index = lax.axis_index("tp")
-    summed = lax.psum(projected, "tp")
+    summed = detail_loads(projected)
     resid_full = lax.all_gather(hidden_in, "tp", axis=1, tiled=True)
     stream = (resid_full.astype(jnp.float32) + summed).astype(jnp.bfloat16)
     stream_f = stream.astype(jnp.float32)

time: 536 us -> 513 us (0.957)
  waiting for transfers between devices: 158 us -> 138 us
  blocking collectives: 96.2 us -> 90.5 us
    psum x1 -> x0, waiting for transfers between devices: 72.6 us -> none  [shards(): summed = lax.psum(projected, 'tp')]
    all_gather x0 -> x1, waiting for transfers between devices: none -> 45.5 us  [detail_loads(): return jax.lax.all_gather(load, axis_name='tp').sum(axis=0)]
    unnamed x48 -> x42, local copies, waits for them, and re-layouts: 77 us -> 77.5 us
  transfers between devices with their start and end apart: 7 -> 7, of which waited for: 6 -> 7; matrix products, arithmetic and copies ran while one was open for 7% -> 7% of each run, Pallas kernels for 0% -> 0%
where the time goes in v1:
time: 513 us; the launch traced here: 510 us
  local copies, waits for them, and re-layouts  164 us (32%)
  waiting for transfers between devices  138 us (27%)
  blocking collectives  90.5 us (18%)
  matrix products  40.9 us (8%)
  other arithmetic  37.2 us (7%)
  starting transfers between devices  25.3 us (5%)
  between operations  14.8 us (3%)
    unnamed x42, local copies, waits for them, and re-layouts  77.5 us
    all_gather x1, waiting for transfers between devices, shards(): every_query = lax.all_gather(queries, 'seq', axis=0, tiled=True)  54.9 us
    all_gather x1, waiting for transfers between devices, detail_loads(): return jax.lax.all_gather(load, axis_name='tp').sum(axis=0)  45.5 us
    all_to_all x1, blocking collectives, shards(): lax.all_to_all(dispatched, 'seq', split_axis=0, concat_axis=0, tiled=True)  45.1 us
    all_gather x1, blocking collectives, shards(): resid_full = lax.all_gather(hidden_in, 'tp', axis=1, tiled=True)  22.7 us
    all_gather x1, blocking collectives, shards(): everyone = lax.all_gather(picked_rows, 'seq', axis=0, tiled=True)  22.6 us
    gather x8, local copies, waits for them, and re-layouts, cache_block(): picked = jnp.take(cache_kv, block_groups, axis=0)  20.7 us
    mul x3, local copies, waits for them, and re-layouts, shards(): shard_scale[..., None]  14.9 us
  transfers between devices with their start and end apart: 7, of which 7 were waited for; matrix products, arithmetic and copies ran while one was open for 7% of the time, Pallas kernels for 0%

profile of v1, /device:TPU:1, one launch (start us, length us, event | category | flops | bytes accessed | tf_op | source)
XLA Modules:
  0.0 510.2 jit_solution(799353927532771245)
XLA Ops:
  8.8 54.9 %all-gather.5.cloned.1.call-done = bf16[32,64,512]{2,1,0:T(8,128)(2,1)} async-done(((bf16[1,64,512]{2,1,0:T(8,128)(2,1)}), bf16[32,64,512]{2,1,0:T(8,128)(2,1)}) %all-gather.5.cloned.1.call-update) | async-done | bytes 2097168 | tf_op jit(solution)/shard_map/all_gather | solution.py:100
  63.7 97.3 %while.15 = (s32[]{:T(128)}, bf16[4,8,64,512]{3,2,1,0:T(8,128)(2,1)}, f32[4,8,64,8]{2,3,1,0:T(8,128)}, f32[4,8,64,8]{2,3,1,0:T(8,128)}, s32[4,8]{1,0:T(4,128)S(1...) while((s32[]{:T(128)}, ...), condition=%wide.region_3.4_spmd.clone, body=%wide.region_0.3_spmd.clone.sunk | while | flops 565184128 | bytes 43791872 | solution.py:107
  65.0 2.9 gather_fusion.1
  89.3 2.9 gather_fusion.1
  99.6 2.7 bitcast_reduce_fusion.3
  113.7 2.9 gather_fusion.1
  123.9 2.7 bitcast_reduce_fusion.3
  138.0 2.9 gather_fusion.1
  162.7 5.1 all-to-all-start.1
  170.3 4.7 all-to-all-done.1
  175.1 3.9 all-to-all-start
  179.1 7.3 %all-to-all-done = f32[32,1,512]{2,1,0:T(1,128)S(1)} async-done(((f32[32,1,512]{2,1,0:T(1,128)}), f32[32,1,512]{2,1,0:T(1,128)S(1)}, u32[]{:S(2)}, u32[]{:S(2)}) %all-to-all-start) | async-done | bytes 65568 | tf_op jit(solution)/shard_map/all_to_all | solution.py:116
  186.4 4.7 all-to-all-start.2
  202.7 5.9 %mul.135 = f32[32,64,8,64]{3,2,1,0:T(8,128)} broadcast(f32[32,64,8]{2,1,0:T(8,128)} %copy.109), dimensions={0,1,2} | broadcast | bytes 4259840 | tf_op jit(solution)/shard_map/mul | solution.py:148
  208.6 7.5 %mul.136 = f32[32,1,64,512]{3,2,1,0:T(8,128)} reshape(f32[32,64,8,64]{3,2,1,0:T(8,128)} %mul.135) | data formatting | bytes 8388608 | tf_op jit(solution)/shard_map/mul | solution.py:148
  216.1 3.0 all-to-all-done.2
  219.1 3.5 multiply_reduce_fusion
  225.0 22.7 %all-gather.1 = bf16[8,360,64]{1,2,0:T(8,128)(2,1)S(1)} all-gather(bf16[1,360,64]{1,2,0:T(8,128)(2,1)S(1)} %bitcast.320), channel_id=1, replica_groups=mesh['seq'=32,'tp'=8] {'tp'}, dimensions={0}, use_global_device_ids=true | all-gather | bytes 414720 | tf_op jit(solution)/shard_map/all_gather | solution.py:162
  252.4 45.5 %all-gather.7.cloned.1.call-done = f32[512,2880]{1,0:T(8,128)} async-done(((f32[64,2880]{1,0:T(8,128)}), f32[512,2880]{1,0:T(8,128)}) %all-gather.7.cloned.1.call-update) | async-done | bytes 5898256 | tf_op jit(solution)/shard_map/all_gather | solution.py:12
  297.9 4.0 reduce_sum.93
  306.8 4.6 copy.120
  311.4 45.1 %all_to_all.25 = bf16[32,16,2880]{2,1,0:T(8,128)(2,1)S(1)} all-to-all(bf16[32,16,2880]{2,1,0:T(8,128)(2,1)} %bitcast.310), channel_id=1, replica_groups=mesh['seq'=32,'tp'=8] {'seq'}, dimensions={0} | all-to-all | bytes 5898240 | tf_op jit(solution)/shard_map/all_to_all | solution.py:192
  358.1 4.2 fusion.27
  362.4 8.5 %convolution_convert_fusion = bf16[32,16,2880]{2,1,0:T(8,128)(2,1)} fusion(bf16[1,360,2880]{2,1,0:T(8,128)(2,1)} %param.32, bf16[32,16,2880]{2,1,0:T(8,128)(2,1)} %copy-done.2, bf16[1,2,2880,360]{2,3,1,0:T(8,128)(2,1)} %param.31, f32[32,1,16,360]{3,2,0,1:T(8,128)} %fusion.27), kind=kOutput, calls=%fused_computation.40 | convolution fusion | flops 2126315520 | bytes 10989568 | tf_op jit(solution)/shard_map/sexf,efd->sexd/dot_general | solution.py:70
  370.9 21.4 %copy.125 = bf16[32,16,2880]{1,0,2:T(8,128)(2,1)} copy(bf16[32,16,2880]{2,1,0:T(8,128)(2,1)} %convolution_convert_fusion) | data formatting | bytes 5898240
  392.2 39.5 %reshape.750 = bf16[2880,512]{1,0:T(8,128)(2,1)} reshape(bf16[2880,32,16]{2,1,0:T(8,128)(2,1)} %bitcast.307) | data formatting | bytes 5898240
  433.4 22.6 %all_gather.19 = bf16[32,16,1,128]{3,1,2,0:T(8,128)(2,1)S(1)} all-gather(bf16[1,16,1,128]{3,1,2,0:T(8,128)(2,1)S(1)} %bitcast_select_fusion.2), channel_id=1, replica_groups=mesh['seq'=32,'tp'=8] {'seq'}, dimensions={0}, use_global_device_ids=true | all-gather | bytes 135168 | tf_op jit(solution)/shard_map/all_gather | solution.py:209
  456.1 12.7 %reduce-scatter.4.cloned.1.call-done = bf16[360,512]{1,0:T(8,128)(2,1)} async-done(((bf16[2880,512]{1,0:T(8,128)(2,1)}), bf16[360,512]{1,0:T(8,128)(2,1)}) %reduce-scatter.4.cloned.1.call-update) | async-done | bytes 368656
  468.8 4.4 reshape.751
  473.2 5.0 copy.126
  478.2 11.3 %all-to-all-start.4 = ((bf16[32,16,360]{2,1,0:T(8,128)(2,1)}), bf16[32,16,360]{2,1,0:T(8,128)(2,1)S(1)}, u32[]{:S(2)}, u32[]{:S(2)}) async-start(bf16[32,16,360]{2,1,0:T(8,128)(2,1)} %copy.126), calls=%async_computation.4 | async-start | bytes 786432 | tf_op jit(solution)/shard_map/all_to_all | solution.py:199
  491.0 8.7 %all-to-all-done.4 = bf16[32,16,360]{2,1,0:T(8,128)(2,1)S(1)} async-done(((bf16[32,16,360]{2,1,0:T(8,128)(2,1)}), bf16[32,16,360]{2,1,0:T(8,128)(2,1)S(1)}, u32[]{:S(2)}, u32[]{:S(2)}) %all-to-all-start.4) | async-done | bytes 368672 | tf_op jit(solution)/shard_map/all_to_all | solution.py:199
  (189 shorter events, 117.4 us)
Async XLA Ops:
  7.2 215.5 %copy-start = (bf16[512,2880]{0,1:T(8,128)(2,1)S(1)}, bf16[512,2880]{0,1:T(8,128)(2,1)}, u32[]{:S(2)}) copy-start(bf16[512,2880]{0,1:T(8,128)(2,1)} %param.26) | copy-start | bytes 8847364
  7.2 56.5 %all-gather.5.cloned.1.call-start = ((), (), s32[]{:S(2)}) async-start(), calls=%async_computation.6 | async-start | bytes 2162688 | tf_op jit(solution)/shard_map/all_gather | solution.py:100
  78.0 3.0 copy-start.1
  102.3 3.0 copy-start.1
  126.6 3.0 copy-start.1
  150.9 3.0 copy-start.1
  161.0 30.6 %copy-start.6 = (bf16[1,64,512]{2,1,0:T(8,128)(2,1)S(1)}, bf16[1,64,512]{2,1,0:T(8,128)(2,1)}, u32[]{:S(2)}) copy-start(bf16[1,64,512]{2,1,0:T(8,128)(2,1)} %param.19) | copy-start | bytes 196612
  161.0 31.3 %copy-start.7 = (bf16[1,64,1,128]{3,1,2,0:T(8,128)(2,1)S(1)}, bf16[1,64,1,128]{3,1,2,0:T(8,128)(2,1)}, u32[]{:S(2)}) copy-start(bf16[1,64,1,128]{3,1,2,0:T(8,128)(2,1)} %param.20) | copy-start | bytes 49156
  162.7 12.4 %all-to-all-start.1 = ((f32[32,1,512]{2,1,0:T(1,128)}), f32[32,1,512]{2,1,0:T(1,128)S(1)}, u32[]{:S(2)}, u32[]{:S(2)}) async-start(f32[32,1,512]{2,1,0:T(1,128)} %reshape.755), calls=%async_computation.1 | async-start | bytes 131072 | tf_op jit(solution)/shard_map/all_to_all | solution.py:115
  175.1 11.3 %all-to-all-start = ((f32[32,1,512]{2,1,0:T(1,128)}), f32[32,1,512]{2,1,0:T(1,128)S(1)}, u32[]{:S(2)}, u32[]{:S(2)}) async-start(f32[32,1,512]{2,1,0:T(1,128)} %reshape.753), calls=%async_computation | async-start | bytes 131072 | tf_op jit(solution)/shard_map/all_to_all | solution.py:116
  186.4 5.8 %copy-start.8 = (f32[32,1,512]{2,1,0:T(1,128)}, f32[32,1,512]{2,1,0:T(1,128)S(1)}, u32[]{:S(2)}) copy-start(f32[32,1,512]{2,1,0:T(1,128)S(1)} %all-to-all-done) | copy-start | bytes 196612
  186.4 32.7 %all-to-all-start.2 = ((bf16[32,1,64,512]{3,2,1,0:T(8,128)(2,1)}), bf16[32,1,64,512]{3,2,1,0:T(8,128)(2,1)}, u32[]{:S(2)}, u32[]{:S(2)}) async-start(bf16[32,1,64,512]{3,2,1,0:T(8,128)(2,1)} %bitcast.315), calls=%async_computation.2 | async-start | bytes 4194304 | tf_op jit(solution)/shard_map/all_to_all | solution.py:113
  191.1 106.8 %all-gather.7.cloned.1.call-start = ((), (), s32[]{:S(2)}) async-start(), calls=%async_computation.7 | async-start | bytes 6782976 | tf_op jit(solution)/shard_map/all_gather | solution.py:12
  192.3 0.6 copy-start.9
  192.6 0.6 copy-start.10
  216.1 6.6 %copy-start.4 = (f32[64,512]{1,0:T(8,128)S(1)}, f32[64,512]{1,0:T(8,128)}, u32[]{:S(2)}) copy-start(f32[64,512]{1,0:T(8,128)} %reshape.677) | copy-start | bytes 393220
  216.1 6.6 %copy-start.5 = (f32[64,512]{1,0:T(8,128)S(1)}, f32[64,512]{1,0:T(8,128)}, u32[]{:S(2)}) copy-start(f32[64,512]{1,0:T(8,128)} %mul.139) | copy-start | bytes 393220
  222.7 2.0 copy-start.12
  222.7 2.3 copy-start.11
  224.6 244.2 %reduce-scatter.4.cloned.1.call-start = ((), (), s32[]{:S(2)}) async-start(), calls=%async_computation.8 | async-start | bytes 3317760
  297.9 6.3 %copy-start.13 = (f32[2880]{0:T(1024)S(1)}, f32[2880]{0:T(1024)}, u32[]{:S(2)}) copy-start(f32[2880]{0:T(1024)} %param.28) | copy-start | bytes 34564
  303.4 0.8 copy-start.3
  356.5 1.6 copy-start.2
  431.7 0.9 copy-start.16
  431.7 24.2 %copy-start.15 = (s32[32]{0:T(128)S(1)}, s32[32]{0:T(128)}, u32[]{:S(2)}) copy-start(s32[32]{0:T(128)} %param.35) | copy-start | bytes 388
  456.1 33.5 %copy-start.14 = (f32[64,4]{0,1:T(4,128)S(1)}, f32[64,4]{0,1:T(4,128)}, u32[]{:S(2)}) copy-start(f32[64,4]{0,1:T(4,128)} %param.30) | copy-start | bytes 3076
  478.2 21.5 %all-to-all-start.4 = ((bf16[32,16,360]{2,1,0:T(8,128)(2,1)}), bf16[32,16,360]{2,1,0:T(8,128)(2,1)S(1)}, u32[]{:S(2)}, u32[]{:S(2)}) async-start(bf16[32,16,360]{2,1,0:T(8,128)(2,1)} %copy.126), calls=%async_computation.4 | async-start | bytes 786432 | tf_op jit(solution)/shard_map/all_to_all | solution.py:199
Sparse Core Ops, SparseCore 0:
  10.6 53.0 all-gather.4
  224.8 73.0 all-gather.6
  431.9 36.8 reduce-scatter.3
